TPU v7x, 256 devices: a whole 4x4x8 slice. The times are simulated.
256 devices in a mesh: lat: 8 (over z), lon: 32 (over y, x, core).
Axes of the slice: x: 4, y: 4, z: 8, core: 2. Of those that a mesh axis runs over, the one named last changes fastest.
Arguments:
- u_wind: float32 [1440, 32, 128], P('lon', 'lat'), may hold values from -6 to 6
- v_wind: float32 [1440, 32, 128], P('lon', 'lat'), may hold values from -6 to 6
- height: float32 [1440, 32, 128], P('lon', 'lat'), may hold values from -6 to 6
- wave_speed: float32 [128], replicated, may hold values from 0.1 to 0.4
- cutoff: int32 [32], replicated, may hold values from 1 to 720, as said below
Outputs:
- u_next: float32 [1440, 32, 128], P('lon', 'lat')
- v_next: float32 [1440, 32, 128], P('lon', 'lat')
- h_next: float32 [1440, 32, 128], P('lon', 'lat')
Inputs may be any that keep to these rules, and one draw needn't show every extreme that they name: `cutoff`: rows 8 to 23, within 45 degrees of the equator, hold 720, which keeps every wavenumber; the other rows hold smaller values, 1 on the two outermost rows.
All inputs are finite; a program needn't handle non-finite values.
Results may differ from a plain program's by a relative error of at most 0.00005.
Values sent between devices are 32-bit elements; how exact they have to be, the bound alone decides.
No kernel may reach another device: no remote copies, remote signals or barrier semaphores. Data moves between devices by JAX's collectives and lax.ppermute only.
A program may use at most 64 MiB of HBM per device.

v0:
```python
import math

import jax
import jax.numpy as jnp
from jax import lax
from jax.sharding import Mesh
from jax.sharding import PartitionSpec as P

LON = ("lon_0", "lon_1", "lon_2")


coriolis_rate = 0.25


def extended(block, sides, width, periodic):
    for axis, dim in sides:
        count = lax.axis_size(axis)
        forward = [(i, i + 1) for i in range(count - 1)]
        if periodic:
            forward.append((count - 1, 0))
        backward = [(target, source) for source, target in forward]
        low = lax.ppermute(
            lax.slice_in_dim(block, block.shape[dim] - width, None, axis=dim), axis, forward
        )
        high = lax.ppermute(lax.slice_in_dim(block, 0, width, axis=dim), axis, backward)
        block = jnp.concatenate([low, block, high], axis=dim)
    return block


def in_blocks(array, dim, count):
    dims = array.shape
    pieces = array.reshape(*dims[:dim], count, dims[dim] // count, *dims[dim + 1 :])
    return jnp.moveaxis(pieces, dim, 0)


def laid_out(pieces, dim):
    dims = list(pieces.shape[1:])
    dims[dim] *= pieces.shape[0]
    return jnp.moveaxis(pieces, 0, dim).reshape(dims)


def turned_blocks(pieces, axes, sequence):
    inside = pieces.shape[1:]
    whole = pieces.reshape(*(lax.axis_size(a) for a in axes), *inside)
    for k in sequence:
        whole = lax.all_to_all(whole, axes[k], k, k, tiled=True)
    return whole.reshape(-1, *inside)


def two_step_exchange(array, groups, sequence, split_dim, concat_dim):
    count = lax.axis_size(groups[0]) * lax.axis_size(groups[1])
    pieces = in_blocks(array, split_dim, count)
    return laid_out(turned_blocks(pieces, groups, sequence), concat_dim)


def tables(points):
    wavenum = jnp.arange(points // 2 + 1, dtype=jnp.int32)
    lon_ids = jnp.arange(points, dtype=jnp.int32)
    phase = wavenum[:, None] * lon_ids[None, :] % points
    angle = phase.astype(jnp.float32) * (2.0 * math.pi / points)
    weight = (
        jnp.where((wavenum == 0) | (wavenum == points // 2), 1.0, 2.0).astype(jnp.float32) / points
    )
    return (jnp.cos(angle), jnp.sin(angle), wavenum, weight)


def shards(u_wind, v_wind, height, wave_speed, cutoff):
    lon_cells, lat_rows, levels = u_wind.shape
    lat_devs = lax.axis_size("lat")
    points = lon_cells * lax.axis_size(LON)
    total_rows = lat_rows * lat_devs
    band_index = lax.axis_index("lat")
    first_row = band_index * lat_rows
    row_ids = first_row + jnp.arange(lat_rows, dtype=jnp.int32)
    latitude = 0.5 * math.pi - (row_ids.astype(jnp.float32) + 0.5) * (math.pi / total_rows)
    cos_lat = jnp.cos(latitude)[:, None]
    sin_lat = jnp.sin(latitude)[:, None]
    stretch = points / (2.0 * total_rows) / cos_lat
    speed_col = wave_speed[None, None, :]
    cos_table, sin_table, wavenum, weight = tables(points)
    cut_own = lax.dynamic_slice_in_dim(cutoff, first_row, lat_rows)

    def tendency(u_now, v_now, h_now):
        east = extended(jnp.stack([u_now, h_now]), ((LON, 1),), 1, True)
        zonal_u = (east[0, 2:, :, :] - east[0, :-2, :, :]) * 0.5
        zonal_h = (east[1, 2:, :, :] - east[1, :-2, :, :]) * 0.5
        north = extended(jnp.stack([v_now * cos_lat, h_now]), (("lat", 2),), 1, False)
        merid_vc = (north[0, :, :-2, :] - north[0, :, 2:, :]) * 0.5
        merid_h = (north[1, :, :-2, :] - north[1, :, 2:, :]) * 0.5
        tend_u = coriolis_rate * sin_lat * v_now - speed_col * (stretch * zonal_h)
        tend_v = -coriolis_rate * sin_lat * u_now - speed_col * merid_h
        tend_h = -speed_col * (stretch * zonal_u + merid_vc / cos_lat)
        return jnp.stack([tend_u, tend_v, tend_h])

    def circles(tend, cut_rows):
        mode_scale = weight[:, None] * (wavenum[:, None] <= cut_rows[None, :]).astype(jnp.float32)
        whole_circles = lax.all_to_all(tend, LON, split_axis=3, concat_axis=1, tiled=True)
        count, circle_len, columns, level_part = whole_circles.shape
        flat = whole_circles.reshape(count, circle_len, columns * level_part)
        scale_flat = jnp.repeat(mode_scale, level_part, axis=1)
        cos_coef = jnp.einsum("ki,nil->nkl", cos_table, flat, precision=lax.Precision.HIGHEST)
        sin_coef = jnp.einsum("ki,nil->nkl", sin_table, flat, precision=lax.Precision.HIGHEST)
        smooth = jnp.einsum(
            "ki,nkl->nil", cos_table, cos_coef * scale_flat, precision=lax.Precision.HIGHEST
        )
        smooth = smooth + jnp.einsum(
            "ki,nkl->nil", sin_table, sin_coef * scale_flat, precision=lax.Precision.HIGHEST
        )
        smooth = smooth.reshape(count, circle_len, columns, level_part)
        return two_step_exchange(smooth, (("lon_0", "lon_1"), "lon_2"), (1, 0), 1, 3)

    def filtered(tend):
        return circles(tend, cut_own)

    fields = (u_wind, v_wind, height)
    change = filtered(tendency(u_wind, v_wind, height))
    first = [fields[n] + change[n] for n in range(3)]
    change = filtered(tendency(first[0], first[1], first[2]))
    second = [0.75 * fields[n] + 0.25 * (first[n] + change[n]) for n in range(3)]
    change = filtered(tendency(second[0], second[1], second[2]))
    third = [1.0 / 3.0 * fields[n] + 2.0 / 3.0 * (second[n] + change[n]) for n in range(3)]
    return (third[0], third[1], third[2])


def solution(mesh):
    split = Mesh(
        mesh.devices.reshape(mesh.shape["lat"], 4, 4, 2), ("lat", "lon_0", "lon_1", "lon_2")
    )
    return jax.shard_map(
        shards,
        mesh=split,
        in_specs=(P(LON, "lat", None), P(LON, "lat", None), P(LON, "lat", None), P(), P()),
        out_specs=(P(LON, "lat", None), P(LON, "lat", None), P(LON, "lat", None)),
        check_vma=False,
    )
```

profile of v0, /device:TPU:97, one launch (start us, length us, event | category | flops | bytes accessed | tf_op | source)
XLA Modules:
  0.0 445.5 jit_solution(16987381019460181)
XLA Ops:
  5.1 2.6 collective-permute-done
  8.2 1.9 collective-permute-start.3
  10.1 4.8 %collective-permute-start.2 = (f32[2,45,1,128]{1,3,2,0:T(8,128)S(1)}, f32[2,45,1,128]{1,3,2,0:T(8,128)S(1)}, u32[]{:S(2)}, u32[]{:S(2)}) collective-permute-start(f32[2,45,1,128]{1,3,2,0:T(8,128)S(1)} %get-tuple-element.32), channel_id=1, source_target_pairs={{0,32},{32,64},{64,96},{96,128},{128,160},{160,192},{192,224},{1,3... | collective-permute-start | bytes 138248 | tf_op jit(solution)/shard_map/ppermute | solution.py:22
  17.7 1.8 reshape.113
  19.5 8.9 %all-to-all-start = ((f32[32,1,2160]{2,1,0:T(1,128)}), f32[32,1,2160]{2,1,0:T(1,128)S(1)}, u32[]{:S(2)}, u32[]{:S(2)}) async-start(f32[32,1,2160]{2,1,0:T(1,128)} %reshape.113), calls=%async_computation | async-start | bytes 557056 | tf_op jit(solution)/shard_map/all_to_all | solution.py:97
  28.6 8.7 %all-to-all-done = f32[32,1,2160]{2,1,0:T(1,128)S(1)} async-done(((f32[32,1,2160]{2,1,0:T(1,128)}), f32[32,1,2160]{2,1,0:T(1,128)S(1)}, u32[]{:S(2)}, u32[]{:S(2)}) %all-to-all-start) | async-done | bytes 276512 | tf_op jit(solution)/shard_map/all_to_all | solution.py:97
  40.8 19.8 %fusion.121 = f32[3,721,16]{1,2,0:T(8,128)S(1)} fusion(f32[3,1440,16]{1,2,0:T(8,128)S(1)} %reshape.102, f32[721,16]{0,1:T(8,128)S(1)} %mul.472), kind=kOutput, calls=%fused_computation.71 | convolution fusion | flops 607404992 | bytes 461056 | tf_op jit(solution)/shard_map/ki,nil->nkl/dot_general | solution.py:102
  60.6 20.6 %fusion.130 = f32[3,721,16]{1,2,0:T(8,128)S(1)} fusion(f32[3,1440,16]{1,2,0:T(8,128)S(1)} %reshape.102, f32[721,16]{0,1:T(8,128)S(1)} %mul.472), kind=kOutput, calls=%fused_computation.74 | convolution fusion | flops 607404992 | bytes 461056 | tf_op jit(solution)/shard_map/ki,nil->nkl/dot_general | solution.py:101
  81.2 21.2 %fusion.10 = f32[3,16,1440]{2,1,0:T(8,128)S(1)} fusion(f32[3,721,16]{1,2,0:T(8,128)S(1)} %fusion.121), kind=kOutput, calls=%fused_computation.11 | convolution fusion | flops 607370368 | bytes 414912 | tf_op jit(solution)/shard_map/ki,nkl->nil/dot_general | solution.py:106
  102.4 21.5 %fusion.58 = f32[3,1440,16]{1,2,0:T(8,128)S(1)} fusion(f32[3,16,1440]{2,1,0:T(8,128)S(1)} %fusion.10, f32[3,721,16]{1,2,0:T(8,128)S(1)} %fusion.130), kind=kOutput, calls=%fused_computation.38 | convolution fusion | flops 607439488 | bytes 691392 | tf_op jit(solution)/shard_map/ki,nkl->nil/dot_general | solution.py:103
  126.6 3.7 all_to_all.75
  134.4 11.5 %all_to_all.76 = f32[16,1,4320]{2,1,0:T(1,128)S(1)} all-to-all(f32[16,1,4320]{2,1,0:T(1,128)S(1)} %reshape.117), channel_id=1, replica_groups=mesh['lat'=8,'lon_0'=4,'lon_1'=4,'lon_2'=2] {'lon_0','lon_1'}, dimensions={0} | all-to-all | bytes 552960 | tf_op jit(solution)/shard_map/all_to_all | solution.py:46
  152.1 2.3 collective-permute-done.4
  155.0 1.9 collective-permute-start.7
  156.9 5.0 %collective-permute-start.6 = (f32[2,45,1,128]{1,3,2,0:T(8,128)S(1)}, f32[2,45,1,128]{1,3,2,0:T(8,128)S(1)}, u32[]{:S(2)}, u32[]{:S(2)}) collective-permute-start(f32[2,45,1,128]{1,3,2,0:T(8,128)S(1)} %get-tuple-element.30), channel_id=1, source_target_pairs={{0,32},{32,64},{64,96},{96,128},{128,160},{160,192},{192,224},{1,3... | collective-permute-start | bytes 138248 | tf_op jit(solution)/shard_map/ppermute | solution.py:22
  165.8 18.7 %all_to_all.77 = f32[32,1,2160]{2,1,0:T(1,128)S(1)} all-to-all(f32[32,1,2160]{2,1,0:T(1,128)S(1)} %reshape.119), channel_id=1, replica_groups=mesh['lat'=8,'lon_0'=4,'lon_1'=4,'lon_2'=2] {'lon_0','lon_1','lon_2'}, dimensions={0} | all-to-all | bytes 552960 | tf_op jit(solution)/shard_map/all_to_all | solution.py:97
  187.5 19.8 %fusion.118 = f32[3,721,16]{1,2,0:T(8,128)S(1)} fusion(f32[3,1440,16]{1,2,0:T(8,128)S(1)} %reshape.105, f32[721,16]{0,1:T(8,128)S(1)} %mul.472), kind=kOutput, calls=%fused_computation.70 | convolution fusion | flops 607404992 | bytes 461056 | tf_op jit(solution)/shard_map/ki,nil->nkl/dot_general | solution.py:102
  207.3 20.4 %fusion.127 = f32[3,721,16]{1,2,0:T(8,128)S(1)} fusion(f32[3,1440,16]{1,2,0:T(8,128)S(1)} %reshape.105, f32[721,16]{0,1:T(8,128)S(1)} %mul.472), kind=kOutput, calls=%fused_computation.73 | convolution fusion | flops 607404992 | bytes 461056 | tf_op jit(solution)/shard_map/ki,nil->nkl/dot_general | solution.py:101
  227.7 21.2 %fusion.6 = f32[3,16,1440]{2,1,0:T(8,128)S(1)} fusion(f32[3,721,16]{1,2,0:T(8,128)S(1)} %fusion.118), kind=kOutput, calls=%fused_computation.7 | convolution fusion | flops 607370368 | bytes 414912 | tf_op jit(solution)/shard_map/ki,nkl->nil/dot_general | solution.py:106
  248.9 21.5 %fusion.55 = f32[3,1440,16]{1,2,0:T(8,128)S(1)} fusion(f32[3,16,1440]{2,1,0:T(8,128)S(1)} %fusion.6, f32[3,721,16]{1,2,0:T(8,128)S(1)} %fusion.127), kind=kOutput, calls=%fused_computation.37 | convolution fusion | flops 607439488 | bytes 691392 | tf_op jit(solution)/shard_map/ki,nkl->nil/dot_general | solution.py:103
  273.1 3.7 all_to_all.78
  280.9 11.5 %all_to_all.79 = f32[16,1,4320]{2,1,0:T(1,128)S(1)} all-to-all(f32[16,1,4320]{2,1,0:T(1,128)S(1)} %reshape.123), channel_id=1, replica_groups=mesh['lat'=8,'lon_0'=4,'lon_1'=4,'lon_2'=2] {'lon_0','lon_1'}, dimensions={0} | all-to-all | bytes 552960 | tf_op jit(solution)/shard_map/all_to_all | solution.py:46
  298.9 2.3 collective-permute-done.8
  301.8 1.9 collective-permute-start.11
  303.8 5.0 %collective-permute-start.10 = (f32[2,45,1,128]{1,3,2,0:T(8,128)S(1)}, f32[2,45,1,128]{1,3,2,0:T(8,128)S(1)}, u32[]{:S(2)}, u32[]{:S(2)}) collective-permute-start(f32[2,45,1,128]{1,3,2,0:T(8,128)S(1)} %get-tuple-element.28), channel_id=1, source_target_pairs={{0,32},{32,64},{64,96},{96,128},{128,160},{160,192},{192,224},{1,3... | collective-permute-start | bytes 138248 | tf_op jit(solution)/shard_map/ppermute | solution.py:22
  312.6 18.7 %all_to_all.80 = f32[32,1,2160]{2,1,0:T(1,128)S(1)} all-to-all(f32[32,1,2160]{2,1,0:T(1,128)S(1)} %reshape.125), channel_id=1, replica_groups=mesh['lat'=8,'lon_0'=4,'lon_1'=4,'lon_2'=2] {'lon_0','lon_1','lon_2'}, dimensions={0} | all-to-all | bytes 552960 | tf_op jit(solution)/shard_map/all_to_all | solution.py:97
  334.4 19.8 %fusion.115 = f32[3,721,16]{1,2,0:T(8,128)S(1)} fusion(f32[3,1440,16]{1,2,0:T(8,128)S(1)} %reshape.108, f32[721,16]{0,1:T(8,128)S(1)} %mul.472), kind=kOutput, calls=%fused_computation.69 | convolution fusion | flops 607404992 | bytes 461056 | tf_op jit(solution)/shard_map/ki,nil->nkl/dot_general | solution.py:102
  354.2 20.4 %fusion.124 = f32[3,721,16]{1,2,0:T(8,128)S(1)} fusion(f32[3,1440,16]{1,2,0:T(8,128)S(1)} %reshape.108, f32[721,16]{0,1:T(8,128)S(1)} %mul.472), kind=kOutput, calls=%fused_computation.72 | convolution fusion | flops 607404992 | bytes 461056 | tf_op jit(solution)/shard_map/ki,nil->nkl/dot_general | solution.py:101
  374.6 21.2 %fusion.2 = f32[3,16,1440]{2,1,0:T(8,128)S(1)} fusion(f32[3,721,16]{1,2,0:T(8,128)S(1)} %fusion.115), kind=kOutput, calls=%fused_computation.3 | convolution fusion | flops 607370368 | bytes 414912 | tf_op jit(solution)/shard_map/ki,nkl->nil/dot_general | solution.py:106
  395.8 21.5 %fusion.52 = f32[3,1440,16]{1,2,0:T(8,128)S(1)} fusion(f32[3,16,1440]{2,1,0:T(8,128)S(1)} %fusion.2, f32[3,721,16]{1,2,0:T(8,128)S(1)} %fusion.124), kind=kOutput, calls=%fused_computation.36 | convolution fusion | flops 607439488 | bytes 691392 | tf_op jit(solution)/shard_map/ki,nkl->nil/dot_general | solution.py:103
  419.9 3.7 all_to_all.81
  427.8 11.5 %all_to_all.82 = f32[16,1,4320]{2,1,0:T(1,128)S(1)} all-to-all(f32[16,1,4320]{2,1,0:T(1,128)S(1)} %reshape.129), channel_id=1, replica_groups=mesh['lat'=8,'lon_0'=4,'lon_1'=4,'lon_2'=2] {'lon_0','lon_1'}, dimensions={0} | all-to-all | bytes 552960 | tf_op jit(solution)/shard_map/all_to_all | solution.py:46
  (156 shorter events, 65.0 us)
Async XLA Ops:
  0.6 7.0 %copy-start.4 = (f32[45,4,128]{2,1,0:T(4,128)S(1)}, f32[45,4,128]{2,1,0:T(4,128)}, u32[]{:S(2)}) copy-start(f32[45,4,128]{2,1,0:T(4,128)} %param.5) | copy-start | bytes 276484
  0.6 3.8 copy-start.6
  0.7 3.8 copy-start.5
  2.6 2.5 collective-permute-start.1
  4.3 3.3 collective-permute-start
  8.2 7.2 %collective-permute-start.3 = (f32[2,45,1,128]{1,3,2,0:T(8,128)S(1)}, f32[2,45,1,128]{1,3,2,0:T(8,128)S(1)}, u32[]{:S(2)}, u32[]{:S(2)}) collective-permute-start(f32[2,45,1,128]{1,3,2,0:T(8,128)S(1)} %get-tuple-element.33), channel_id=1, source_target_pairs={{32,0},{64,32},{96,64},{128,96},{160,128},{192,160},{224,192},{33,... | collective-permute-start | bytes 138248 | tf_op jit(solution)/shard_map/ppermute | solution.py:25
  10.1 6.7 %collective-permute-start.2 = (f32[2,45,1,128]{1,3,2,0:T(8,128)S(1)}, f32[2,45,1,128]{1,3,2,0:T(8,128)S(1)}, u32[]{:S(2)}, u32[]{:S(2)}) collective-permute-start(f32[2,45,1,128]{1,3,2,0:T(8,128)S(1)} %get-tuple-element.32), channel_id=1, source_target_pairs={{0,32},{32,64},{64,96},{96,128},{128,160},{160,192},{192,224},{1,3... | collective-permute-start | bytes 138248 | tf_op jit(solution)/shard_map/ppermute | solution.py:22
  17.7 10.7 %copy-start.7 = (s32[32]{0:T(128)S(1)}, s32[32]{0:T(128)}, u32[]{:S(2)}) copy-start(s32[32]{0:T(128)} %param.9) | copy-start | bytes 388
  19.5 17.8 %all-to-all-start = ((f32[32,1,2160]{2,1,0:T(1,128)}), f32[32,1,2160]{2,1,0:T(1,128)S(1)}, u32[]{:S(2)}, u32[]{:S(2)}) async-start(f32[32,1,2160]{2,1,0:T(1,128)} %reshape.113), calls=%async_computation | async-start | bytes 557056 | tf_op jit(solution)/shard_map/all_to_all | solution.py:97
  149.6 2.5 collective-permute-start.5
  151.3 3.0 collective-permute-start.4
  155.0 7.3 %collective-permute-start.7 = (f32[2,45,1,128]{1,3,2,0:T(8,128)S(1)}, f32[2,45,1,128]{1,3,2,0:T(8,128)S(1)}, u32[]{:S(2)}, u32[]{:S(2)}) collective-permute-start(f32[2,45,1,128]{1,3,2,0:T(8,128)S(1)} %get-tuple-element.31), channel_id=1, source_target_pairs={{32,0},{64,32},{96,64},{128,96},{160,128},{192,160},{224,192},{33,... | collective-permute-start | bytes 138248 | tf_op jit(solution)/shard_map/ppermute | solution.py:25
  156.9 6.9 %collective-permute-start.6 = (f32[2,45,1,128]{1,3,2,0:T(8,128)S(1)}, f32[2,45,1,128]{1,3,2,0:T(8,128)S(1)}, u32[]{:S(2)}, u32[]{:S(2)}) collective-permute-start(f32[2,45,1,128]{1,3,2,0:T(8,128)S(1)} %get-tuple-element.30), channel_id=1, source_target_pairs={{0,32},{32,64},{64,96},{96,128},{128,160},{160,192},{192,224},{1,3... | collective-permute-start | bytes 138248 | tf_op jit(solution)/shard_map/ppermute | solution.py:22
  295.8 0.7 copy-start
  296.5 2.4 collective-permute-start.9
  298.2 3.0 collective-permute-start.8
  301.7 7.2 %copy-start.2 = (f32[45,4,128]{0,2,1:T(8,128)}, f32[45,4,128]{0,2,1:T(8,128)S(1)}, u32[]{:S(2)}) copy-start(f32[45,4,128]{0,2,1:T(8,128)S(1)} %get-tuple-element.16) | copy-start | bytes 276484
  301.8 7.3 %collective-permute-start.11 = (f32[2,45,1,128]{1,3,2,0:T(8,128)S(1)}, f32[2,45,1,128]{1,3,2,0:T(8,128)S(1)}, u32[]{:S(2)}, u32[]{:S(2)}) collective-permute-start(f32[2,45,1,128]{1,3,2,0:T(8,128)S(1)} %get-tuple-element.29), channel_id=1, source_target_pairs={{32,0},{64,32},{96,64},{128,96},{160,128},{192,160},{224,192},{33,... | collective-permute-start | bytes 138248 | tf_op jit(solution)/shard_map/ppermute | solution.py:25
  303.8 6.9 %collective-permute-start.10 = (f32[2,45,1,128]{1,3,2,0:T(8,128)S(1)}, f32[2,45,1,128]{1,3,2,0:T(8,128)S(1)}, u32[]{:S(2)}, u32[]{:S(2)}) collective-permute-start(f32[2,45,1,128]{1,3,2,0:T(8,128)S(1)} %get-tuple-element.28), channel_id=1, source_target_pairs={{0,32},{32,64},{64,96},{96,128},{128,160},{160,192},{192,224},{1,3... | collective-permute-start | bytes 138248 | tf_op jit(solution)/shard_map/ppermute | solution.py:22
  442.4 1.0 copy-start.3
  443.4 1.0 copy-start.1
where the time goes:
time: 451 us; the launch traced here: 446 us
  matrix products  249 us (55%)
  blocking collectives  83.1 us (18%)
  local copies, waits for them, and re-layouts  39.9 us (9%)
  starting transfers between devices  34.6 us (8%)
  waiting for transfers between devices  22.1 us (5%)
  other arithmetic  15.3 us (3%)
    dot_general x3, matrix products, circles(): jnp.einsum('ki,nkl->nil', cos_table, cos_coef * scale_flat, precision=lax...  64.4 us
    dot_general x3, matrix products, circles(): jnp.einsum('ki,nkl->nil', sin_table, sin_coef * scale_flat, precision=lax...  63.5 us
    dot_general x3, matrix products, circles(): jnp.einsum('ki,nil->nkl', cos_table, flat, precision=lax.Precision.HIGHEST)  61.4 us
    dot_general x3, matrix products, circles(): jnp.einsum('ki,nil->nkl', sin_table, flat, precision=lax.Precision.HIGHEST)  59.4 us
    all_to_all x6, blocking collectives, turned_blocks(): whole = lax.all_to_all(whole, axes[k], k, k, tiled=True)  45.7 us
    all_to_all x2, blocking collectives, circles(): lax.all_to_all(tend, LON, split_axis=3, concat_axis=1, tiled=True)  37.4 us
    unnamed x55, local copies, waits for them, and re-layouts  27.7 us
    ppermute x6, starting transfers between devices, extended(): lax.ppermute(lax.slice_in_dim(block, block.shape[dim] - width, None, axis...  19.9 us
  transfers between devices with their start and end apart: 13, of which 12 were waited for; matrix products, arithmetic and copies ran while one was open for 0% of the time, Pallas kernels for 0%

commit v1 on v0

v1 whole, which is shorter than its diff:
```python
import functools
import math

import jax
import jax.numpy as jnp
import numpy as np
from jax import lax
from jax.experimental import pallas as pl
from jax.experimental.pallas import tpu as pltpu
from jax.sharding import Mesh
from jax.sharding import PartitionSpec as P

LON = ("lon_0", "lon_1", "lon_2")

NB = 32
NR = 45
PTS = NB * NR
NK = NB // 2 + 1
ST = 48
ROWS = 4
HALO = 3
LV = 4
OWN = ROWS * ST
WIDE = 512
UP0 = WIDE - HALO * ST
DN1 = OWN + HALO * ST
PACK = 8 * ST
HI = lax.Precision.HIGHEST


def host_tables(bands):
    r = np.arange(NR)
    ang = 2.0 * np.pi * np.outer(r, r) / NR
    fwd_c = np.zeros((OWN, 256))
    fwd_s = np.zeros((OWN, 256))
    inv_c = np.zeros((256, OWN))
    inv_s = np.zeros((256, OWN))
    for j in range(ROWS):
        at = slice(j * ST, j * ST + NR)
        fwd_c[at, at] = np.cos(ang)
        fwd_s[at, at] = np.sin(ang)
        inv_c[at, at] = np.cos(ang) / PTS
        inv_s[at, at] = np.sin(ang) / PTS
    twid = np.zeros((NK, 2, OWN))
    for k in range(NK):
        for j in range(ROWS):
            at = slice(j * ST, j * ST + NR)
            twid[k, 0, at] = np.cos(2.0 * np.pi * k * r / PTS)
            twid[k, 1, at] = np.sin(2.0 * np.pi * k * r / PTS)
    row_of = np.full(WIDE, -100)
    k2_of = np.zeros(WIDE, np.int64)
    for row in range(-HALO, ROWS + HALO):
        first = row * ST if row >= 0 else WIDE + row * ST
        row_of[first : first + NR] = row
        k2_of[first : first + NR] = r
    wav = np.arange(NK)[:, None] + NB * k2_of[None, :]
    slope = np.sin(2.0 * np.pi * wav / PTS)
    least = np.minimum(wav, PTS - wav)
    total = bands * ROWS
    per_band = np.zeros((bands, 4, WIDE))
    for z in range(bands):
        g = z * ROWS + row_of
        ok = (g >= 0) & (g < total) & (row_of > -100)
        half_pi = np.float32(0.5 * math.pi)
        lat = half_pi - (g.astype(np.float32) + np.float32(0.5)) * np.float32(math.pi / total)
        cos = np.cos(lat, dtype=np.float32)
        sin = np.sin(lat, dtype=np.float32)
        cos = np.where(ok, cos, 1.0)
        per_band[z, 0] = np.where(ok, 0.25 * sin, 0.0)
        per_band[z, 1] = np.where(ok, PTS / (2.0 * total) / cos, 0.0)
        per_band[z, 2] = np.where(ok, cos, 0.0)
        per_band[z, 3] = np.where(ok, 0.5 / cos, 0.0)
    f32 = lambda a: jnp.asarray(np.asarray(a, np.float32))
    return (
        tuple(f32(a) for a in (fwd_c, fwd_s, inv_c, inv_s, twid, slope[:, None, :], per_band)),
        jnp.asarray(least[:, None, :].astype(np.int32)),
    )


def real_fft(xs):
    n = len(xs)
    if n == 1:
        return [(xs[0], None)]
    even, odd = real_fft(xs[0::2]), real_fft(xs[1::2])
    out = [None] * (n // 2 + 1)
    for k in range(n // 4 + 1 if n > 2 else 1):
        er, ei = even[k]
        orr, oi = odd[k]
        if k == 0:
            out[0] = (er + orr, None)
            out[n // 2] = (er - orr, None)
        elif 4 * k == n:
            out[k] = (er, -orr)
        else:
            c, s = math.cos(2 * math.pi * k / n), math.sin(2 * math.pi * k / n)
            if oi is None:
                tr, ti = orr * c, orr * (-s)
            elif 8 * k == n:
                tr, ti = (orr + oi) * c, (oi - orr) * c
            else:
                tr, ti = orr * c + oi * s, oi * c - orr * s
            if ei is None:
                out[k] = (er + tr, ti)
                out[n // 2 - k] = (er - tr, ti)
            else:
                out[k] = (er + tr, ei + ti)
                out[n // 2 - k] = (er - tr, ti - ei)
    return out


def real_ifft(spec):
    n = 2 * (len(spec) - 1)
    if n == 2:
        return [spec[0][0] + spec[1][0], spec[0][0] - spec[1][0]]
    even, odd = [None] * (n // 4 + 1), [None] * (n // 4 + 1)
    for k in range(n // 4 + 1):
        ar, ai = spec[k]
        if k == 0:
            br = spec[n // 2][0]
            even[0] = (ar + br, None)
            odd[0] = (ar - br, None)
        elif 4 * k == n:
            even[k] = (2.0 * ar, None)
            odd[k] = (-2.0 * ai, None)
        else:
            br, bi = spec[n // 2 - k]
            even[k] = (ar + br, ai - bi)
            dr, di = ar - br, ai + bi
            c, s = math.cos(2 * math.pi * k / n), math.sin(2 * math.pi * k / n)
            if 8 * k == n:
                odd[k] = ((dr - di) * c, (dr + di) * c)
            else:
                odd[k] = (dr * c - di * s, dr * s + di * c)
    xe, xo = real_ifft(even), real_ifft(odd)
    out = []
    for a, b in zip(xe, xo):
        out += [a, b]
    return out


def pack_kernel(u_ref, v_ref, h_ref, o_ref, tmp):
    tmp[...] = jnp.zeros_like(tmp)
    for f, ref in enumerate((u_ref, v_ref, h_ref)):
        for j in range(ROWS):
            tmp[f, j * ST : j * ST + NR, :] = ref[:, j, :]
    for f in range(3):
        turned = tmp[f].T
        for l in range(LV):
            o_ref[:, f, l, :] = turned[l * NB : (l + 1) * NB, :OWN]


def forward_kernel(z_ref, c_ref, s_ref, tw_ref, own_ref, up_ref, dn_ref, x_ref, xi_ref):
    for f in range(3):
        spec = real_fft([z_ref[d, f] for d in range(NB)])
        for k in range(NK):
            a, b = spec[k]
            c, s = tw_ref[k, 0:1, :], tw_ref[k, 1:2, :]
            if b is None:
                re, im = a * c, -(a * s)
            else:
                re, im = a * c + b * s, b * c - a * s
            x_ref[f, k * 8 : k * 8 + 4, :] = re
            x_ref[f, k * 8 + 4 : k * 8 + 8, :] = im
            xi_ref[f, k * 8 : k * 8 + 4, :] = im
            xi_ref[f, k * 8 + 4 : k * 8 + 8, :] = -re
    got = []
    for f in range(3):
        y = jnp.dot(x_ref[f], c_ref[...], precision=HI, preferred_element_type=jnp.float32)
        y = y + jnp.dot(xi_ref[f], s_ref[...], precision=HI, preferred_element_type=jnp.float32)
        own_ref[f] = y
    for k in range(NK):
        at = slice(k * 8, k * 8 + 8)
        pad = jnp.zeros((8, 128), jnp.float32)
        u, v, h = (jnp.concatenate([own_ref[f, at, :], pad], axis=1) for f in range(3))
        lane = lax.broadcasted_iota(jnp.int32, (8, PACK), 1)
        roll = lambda a, n: pltpu.roll(a, n % PACK, 1)
        up_ref[at, :] = jnp.where(
            lane < 2 * ST, roll(u, -2 * ST), jnp.where(lane < 5 * ST, roll(v, ST), roll(h, 4 * ST))
        )
        dn_ref[at, :] = jnp.where(
            lane < 2 * ST, u, jnp.where(lane < 5 * ST, roll(v, 2 * ST), roll(h, 5 * ST))
        )


def step_kernel(
    cut_ref, speed_ref, own_ref, up_ref, dn_ref, slope_ref, least_ref, band_ref,
    c_ref, s_ref, tw_ref, w_ref, y_ref, pc_ref, ps_ref,
):
    z = lax.axis_index("lat")
    p = (lax.axis_index("lon_0") * 4 + lax.axis_index("lon_1")) * 2 + lax.axis_index("lon_2")
    total = cut_ref.shape[0]
    lane1 = lax.broadcasted_iota(jnp.int32, (1, WIDE), 1)
    cut = jnp.full((1, WIDE), -1, jnp.int32)
    for row in range(-HALO, ROWS + HALO):
        g = z * ROWS + row
        inside = jnp.logical_and(g >= 0, g < total)
        value = jnp.where(inside, cut_ref[jnp.clip(g, 0, total - 1)], -1)
        first = row * ST if row >= 0 else WIDE + row * ST
        cut = jnp.where(jnp.logical_and(lane1 >= first, lane1 < first + NR), value, cut)
    sub = lax.broadcasted_iota(jnp.int32, (8, WIDE), 0)
    lane = lax.broadcasted_iota(jnp.int32, (8, WIDE), 1)
    speed = jnp.zeros((8, WIDE), jnp.float32)
    for l in range(LV):
        speed = jnp.where(sub % LV == l, speed_ref[l * NB + p], speed)
    turn_speed = jnp.where(sub < LV, -speed, speed)
    cor = band_ref[z, 0:1, :]
    stretch = band_ref[z, 1:2, :]
    cosl = band_ref[z, 2:3, :]
    half_sec = band_ref[z, 3:4, :]
    roll = lambda a, n: pltpu.roll(a, n % WIDE, 1)

    def body(k, carry):
        at = pl.ds(pl.multiple_of(k * 8, 8), 8)
        up = jnp.concatenate([up_ref[at, :], jnp.zeros((8, 128), jnp.float32)], axis=1)
        dn = jnp.concatenate([dn_ref[at, :], jnp.zeros((8, 128), jnp.float32)], axis=1)
        fields = []
        for f, (up_by, dn_by, n) in enumerate(
            ((-2 * ST, 4 * ST, 2), (-5 * ST, 2 * ST, 3), (-8 * ST, -ST, 3))
        ):
            own = jnp.concatenate([own_ref[f, at, :], jnp.zeros((8, 256), jnp.float32)], axis=1)
            q = jnp.where(lane >= WIDE - n * ST, roll(up, up_by), own)
            q = jnp.where(jnp.logical_and(lane >= OWN, lane < OWN + n * ST), roll(dn, dn_by), q)
            fields.append(q)
        keep = least_ref[k] <= cut
        zs = slope_ref[k] * stretch

        def apply(u, v, h):
            su = pltpu.roll(u, LV, 0)
            sh = pltpu.roll(h, LV, 0)
            vc = v * cosl
            dh = (roll(h, ST) - roll(h, -ST)) * 0.5
            dv = (roll(vc, ST) - roll(vc, -ST)) * half_sec
            tu = cor * v - turn_speed * (zs * sh)
            tv = -(cor * u) - speed * dh
            th = -(turn_speed * (zs * su)) - speed * dv
            return tuple(jnp.where(keep, t, 0.0) for t in (tu, tv, th))

        change = apply(*fields)
        first = [q + t for q, t in zip(fields, change)]
        change = apply(*first)
        second = [0.75 * q + 0.25 * (a + t) for q, a, t in zip(fields, first, change)]
        change = apply(*second)
        for f in range(3):
            gain = jnp.where(keep, second[f] - fields[f], 0.0) + change[f]
            y_ref[f, at, :] = (2.0 / 3.0) * gain[:, :256]
        return carry

    lax.fori_loop(0, NK, body, 0)
    for f in range(3):
        pc_ref[f] = jnp.dot(y_ref[f], c_ref[...], precision=HI, preferred_element_type=jnp.float32)
        ps_ref[f] = jnp.dot(y_ref[f], s_ref[...], precision=HI, preferred_element_type=jnp.float32)
    for f in range(3):
        spec = []
        for k in range(NK):
            re, im = slice(k * 8, k * 8 + 4), slice(k * 8 + 4, k * 8 + 8)
            a = pc_ref[f, re, :] - ps_ref[f, im, :]
            b = pc_ref[f, im, :] + ps_ref[f, re, :]
            c, s = tw_ref[k, 0:1, :], tw_ref[k, 1:2, :]
            spec.append((a * c - b * s, a * s + b * c))
        for d, value in enumerate(real_ifft(spec)):
            w_ref[d, f] = value


def unpack_kernel(w_ref, u_ref, v_ref, h_ref, uo_ref, vo_ref, ho_ref):
    for f, (ref, out) in enumerate(((u_ref, uo_ref), (v_ref, vo_ref), (h_ref, ho_ref))):
        block = jnp.concatenate([w_ref[:, f, l, :] for l in range(LV)], axis=0)
        turned = block.T
        for j in range(ROWS):
            out[:, j, :] = ref[:, j, :] + turned[j * ST : j * ST + NR, :]


def vmem(count):
    return [pl.BlockSpec(memory_space=pltpu.VMEM)] * count


def smem(count):
    return [pl.BlockSpec(memory_space=pltpu.SMEM)] * count


def shaped(*dims):
    return jax.ShapeDtypeStruct(dims, jnp.float32)


def shards(u_wind, v_wind, height, wave_speed, cutoff):
    bands = lax.axis_size("lat")
    (fwd_c, fwd_s, inv_c, inv_s, twid, slope, per_band), least = host_tables(bands)
    packed = pl.pallas_call(
        pack_kernel,
        out_shape=shaped(NB, 3, LV, OWN),
        in_specs=vmem(3),
        out_specs=vmem(1)[0],
        scratch_shapes=[pltpu.VMEM((3, 256, 128), jnp.float32)],
        name="pack",
    )(u_wind, v_wind, height)
    circles = lax.all_to_all(packed, LON, 0, 0, tiled=True)
    own, up, dn = pl.pallas_call(
        forward_kernel,
        out_shape=(shaped(3, NK * 8, 256), shaped(NK * 8, PACK), shaped(NK * 8, PACK)),
        in_specs=vmem(4),
        out_specs=tuple(vmem(3)),
        scratch_shapes=[pltpu.VMEM((3, NK * 8, OWN), jnp.float32)] * 2,
        name="forward",
    )(circles, fwd_c, fwd_s, twid)
    south = [(i, i + 1) for i in range(bands - 1)]
    north = [(b, a) for a, b in south]
    up = lax.ppermute(up, "lat", south)
    dn = lax.ppermute(dn, "lat", north)
    waves = pl.pallas_call(
        step_kernel,
        out_shape=shaped(NB, 3, LV, OWN),
        in_specs=smem(2) + vmem(9),
        out_specs=vmem(1)[0],
        scratch_shapes=[pltpu.VMEM((3, NK * 8, 256), jnp.float32)]
        + [pltpu.VMEM((3, NK * 8, OWN), jnp.float32)] * 2,
        name="sections",
    )(cutoff, wave_speed, own, up, dn, slope, least, per_band, inv_c, inv_s, twid)
    waves = lax.all_to_all(waves, LON, 0, 0, tiled=True)
    return pl.pallas_call(
        unpack_kernel,
        out_shape=tuple(shaped(NR, ROWS, u_wind.shape[2]) for _ in range(3)),
        in_specs=vmem(4),
        out_specs=tuple(vmem(3)),
        name="unpack",
    )(waves, u_wind, v_wind, height)


def solution(mesh):
    split = Mesh(
        mesh.devices.reshape(mesh.shape["lat"], 4, 4, 2), ("lat", "lon_0", "lon_1", "lon_2")
    )
    return jax.shard_map(
        shards,
        mesh=split,
        in_specs=(P(LON, "lat", None), P(LON, "lat", None), P(LON, "lat", None), P(), P()),
        out_specs=(P(LON, "lat", None), P(LON, "lat", None), P(LON, "lat", None)),
        check_vma=False,
    )
```

time: 451 us -> 66.5 us (0.15); the launches traced: 446 us -> 66.1 us
  matrix products: 249 us -> 0 us
  blocking collectives: 83.1 us -> 33.9 us
  local copies, waits for them, and re-layouts: 39.9 us -> 0.68 us
  starting transfers between devices: 34.6 us -> 6.67 us
  Pallas kernels: 0 us -> 16.6 us
  other arithmetic: 15.3 us -> 0 us
  waiting for transfers between devices: 22.1 us -> 7.56 us
    dot_general x12 -> x0, matrix products: 249 us -> none  [the longest x3 64.4 us: circles(): jnp.einsum('ki,nkl->nil', cos_table, cos_coef * scale_flat, precision=lax...]
    all_to_all x8 -> x2, blocking collectives: 83.1 us -> 33.9 us  [the longest x1 18 us: shards(): circles = lax.all_to_all(packed, LON, 0, 0, tiled=True)]
    unnamed x55 -> x4, local copies, waits for them, and re-layouts: 27.7 us -> 0.68 us
    ppermute x12 -> x2, starting transfers between devices: 25.7 us -> 6.67 us  [the longest x1 4.75 us: shards(): up = lax.ppermute(up, 'lat', south)]
    pallas_call x0 -> x4, Pallas kernels: none -> 16.6 us  [the longest x1 9.2 us: shards(): pl.pallas_call(step_kernel, out_shape=shaped(NB, 3, LV, OWN), in_specs=sm...]
    all_to_all x9 -> x0, other arithmetic: 12.3 us -> none  [the longest x6 8.37 us: turned_blocks(): whole = lax.all_to_all(whole, axes[k], k, k, tiled=True)]
    all_to_all x1 -> x0, starting transfers between devices: 8.86 us -> none  [circles(): lax.all_to_all(tend, LON, split_axis=3, concat_axis=1, tiled=True)]
    all_to_all x1 -> x0, waiting for transfers between devices: 8.69 us -> none  [circles(): lax.all_to_all(tend, LON, split_axis=3, concat_axis=1, tiled=True)]
  transfers between devices with their start and end apart: 13 -> 2, of which waited for: 12 -> 2; matrix products, arithmetic and copies ran while one was open for 0% -> 0% of each run, Pallas kernels for 0% -> 0%
where the time goes in v1:
time: 66.5 us; the launch traced here: 66.1 us
  blocking collectives  33.9 us (51%)
  Pallas kernels  16.6 us (25%)
  waiting for transfers between devices  7.56 us (11%)
  starting transfers between devices  6.67 us (10%)
  local copies, waits for them, and re-layouts  0.68 us (1%)
    all_to_all x1, blocking collectives, shards(): circles = lax.all_to_all(packed, LON, 0, 0, tiled=True)  18 us
    all_to_all x1, blocking collectives, shards(): waves = lax.all_to_all(waves, LON, 0, 0, tiled=True)  15.9 us
    pallas_call x1, Pallas kernels, shards(): pl.pallas_call(step_kernel, out_shape=shaped(NB, 3, LV, OWN), in_specs=sm...  9.2 us
    ppermute x1, waiting for transfers between devices, shards(): dn = lax.ppermute(dn, 'lat', north)  4.94 us
    ppermute x1, starting transfers between devices, shards(): up = lax.ppermute(up, 'lat', south)  4.75 us
    pallas_call x1, Pallas kernels, shards(): pl.pallas_call(forward_kernel, out_shape=(shaped(3, NK * 8, 256), shaped(...  3.26 us
    ppermute x1, waiting for transfers between devices, shards(): up = lax.ppermute(up, 'lat', south)  2.62 us
    pallas_call x1, Pallas kernels, shards(): pl.pallas_call(unpack_kernel, out_shape=tuple((shaped(NR, ROWS, u_wind.sh...  2.14 us
  transfers between devices with their start and end apart: 2, of which 2 were waited for; matrix products, arithmetic and copies ran while one was open for 0% of the time, Pallas kernels for 0%

profile of v1, /device:TPU:97, one launch (start us, length us, event | category | flops | bytes accessed | tf_op | source)
XLA Modules:
  0.0 66.1 jit_solution(2316121754728959173)
XLA Ops:
  0.6 2.0 %pack.1 = f32[32,3,4,192]{3,2,1,0:T(4,128)} custom-call(f32[45,4,128]{2,1,0:T(4,128)} %u_ref.3, f32[45,4,128]{2,1,0:T(4,128)} %v_ref.3, f32[45,4,128]{2,1,0:T(4,128)} %h_ref.3), custom_call_target="tpu_custom_call" | custom-call | tf_op jit(solution)/shard_map/pack/pallas_call | solution.py:287
  2.6 18.0 %all_to_all.10.z_ref = f32[32,3,4,192]{3,2,1,0:T(4,128)} all-to-all(f32[32,3,4,192]{3,2,1,0:T(4,128)} %pack.1), channel_id=1, replica_groups=mesh['lat'=8,'lon_0'=4,'lon_1'=4,'lon_2'=2] {'lon_0','lon_1','lon_2'}, dimensions={0} | all-to-all | bytes 589824 | tf_op jit(solution)/shard_map/all_to_all | solution.py:295
  20.6 3.3 %forward.1 = (f32[3,136,256]{2,1,0:T(8,128)}, f32[136,384]{1,0:T(8,128)}, f32[136,384]{1,0:T(8,128)}) custom-call(f32[32,3,4,192]{3,2,1,0:T(4,128)} %all_to_all.10.z_ref, f32[192,256]{1,0:T(8,128)} %constant.16.clone.c_ref, f32[192,256]{1,0:T(8,128)} %constant.17.clone.s_ref, f32[17,2,192]{2,1,0:T(2,128)} %constant.20.clone.tw_ref), custom_call_target="tpu_custom_call" | custom-call | tf_op jit(solution)/shard_map/forward/pallas_call | solution.py:296
  23.9 4.8 %collective-permute-start = (f32[136,384]{1,0:T(8,128)}, f32[136,384]{1,0:T(8,128)S(1)}, u32[]{:S(2)}, u32[]{:S(2)}) collective-permute-start(f32[136,384]{1,0:T(8,128)} %get-tuple-element.7), channel_id=1, source_target_pairs={{0,32},{32,64},{64,96},{96,128},{128,160},{160,192},{192,224},{1,3... | collective-permute-start | bytes 626696 | tf_op jit(solution)/shard_map/ppermute | solution.py:306
  28.7 1.9 %collective-permute-start.1 = (f32[136,384]{1,0:T(8,128)}, f32[136,384]{1,0:T(8,128)S(1)}, u32[]{:S(2)}, u32[]{:S(2)}) collective-permute-start(f32[136,384]{1,0:T(8,128)} %get-tuple-element.8), channel_id=1, source_target_pairs={{32,0},{64,32},{96,64},{128,96},{160,128},{192,160},{224,192},{33,... | collective-permute-start | bytes 626696 | tf_op jit(solution)/shard_map/ppermute | solution.py:307
  30.6 2.6 %collective-permute-done.up_ref = f32[136,384]{1,0:T(8,128)S(1)} collective-permute-done((f32[136,384]{1,0:T(8,128)}, f32[136,384]{1,0:T(8,128)S(1)}, u32[]{:S(2)}, u32[]{:S(2)}) %collective-permute-start) | collective-permute-done | bytes 208928 | tf_op jit(solution)/shard_map/ppermute | solution.py:306
  33.2 0.0 copy-start
  33.2 4.9 %collective-permute-done.1.dn_ref = f32[136,384]{1,0:T(8,128)S(1)} collective-permute-done((f32[136,384]{1,0:T(8,128)}, f32[136,384]{1,0:T(8,128)S(1)}, u32[]{:S(2)}, u32[]{:S(2)}) %collective-permute-start.1) | collective-permute-done | bytes 208928 | tf_op jit(solution)/shard_map/ppermute | solution.py:307
  38.1 0.0 copy-start.1
  38.1 0.0 copy-done
  38.2 0.7 %copy-done.1 = f32[136,384]{1,0:T(8,128)} copy-done((f32[136,384]{1,0:T(8,128)}, f32[136,384]{1,0:T(8,128)S(1)}, u32[]{:S(2)}) %copy-start.1) | copy-done | bytes 208920
  38.8 9.2 %sections.1 = f32[32,3,4,192]{3,2,1,0:T(4,128)} custom-call(s32[32]{0:T(128)} %cut_ref.1, f32[128]{0:T(128)} %speed_ref.1, f32[3,136,256]{2,1,0:T(8,128)} %get-tuple-element.6.own_ref, f32[136,384]{1,0:T(8,128)} %copy-done, f32[136,384]{1,0:T(8,128)} %copy-done.1, f32[17,1,512]{2,1,0:T(1,128)} %constant.21.clone.slope_ref, ...), custom_call_target="tpu_custom_call" | custom-call | tf_op jit(solution)/shard_map/sections/pallas_call | solution.py:308
  48.0 15.9 %all_to_all.11.w_ref = f32[32,3,4,192]{3,2,1,0:T(4,128)} all-to-all(f32[32,3,4,192]{3,2,1,0:T(4,128)} %sections.1), channel_id=1, replica_groups=mesh['lat'=8,'lon_0'=4,'lon_1'=4,'lon_2'=2] {'lon_0','lon_1','lon_2'}, dimensions={0} | all-to-all | bytes 589824 | tf_op jit(solution)/shard_map/all_to_all | solution.py:317
  63.9 2.1 %unpack.1 = (f32[45,4,128]{2,1,0:T(4,128)}, f32[45,4,128]{2,1,0:T(4,128)}, f32[45,4,128]{2,1,0:T(4,128)}) custom-call(f32[32,3,4,192]{3,2,1,0:T(4,128)} %all_to_all.11.w_ref, f32[45,4,128]{2,1,0:T(4,128)} %u_ref.3, f32[45,4,128]{2,1,0:T(4,128)} %v_ref.3, f32[45,4,128]{2,1,0:T(4,128)} %h_ref.3), custom_call_target="tpu_custom_call" | custom-call | tf_op jit(solution)/shard_map/unpack/pallas_call | solution.py:318
Async XLA Ops:
  23.9 9.3 %collective-permute-start = (f32[136,384]{1,0:T(8,128)}, f32[136,384]{1,0:T(8,128)S(1)}, u32[]{:S(2)}, u32[]{:S(2)}) collective-permute-start(f32[136,384]{1,0:T(8,128)} %get-tuple-element.7), channel_id=1, source_target_pairs={{0,32},{32,64},{64,96},{96,128},{128,160},{160,192},{192,224},{1,3... | collective-permute-start | bytes 626696 | tf_op jit(solution)/shard_map/ppermute | solution.py:306
  28.7 9.5 %collective-permute-start.1 = (f32[136,384]{1,0:T(8,128)}, f32[136,384]{1,0:T(8,128)S(1)}, u32[]{:S(2)}, u32[]{:S(2)}) collective-permute-start(f32[136,384]{1,0:T(8,128)} %get-tuple-element.8), channel_id=1, source_target_pairs={{32,0},{64,32},{96,64},{128,96},{160,128},{192,160},{224,192},{33,... | collective-permute-start | bytes 626696 | tf_op jit(solution)/shard_map/ppermute | solution.py:307
  33.2 4.9 %copy-start = (f32[136,384]{1,0:T(8,128)}, f32[136,384]{1,0:T(8,128)S(1)}, u32[]{:S(2)}) copy-start(f32[136,384]{1,0:T(8,128)S(1)} %collective-permute-done.up_ref) | copy-start | bytes 626692
  38.1 0.7 %copy-start.1 = (f32[136,384]{1,0:T(8,128)}, f32[136,384]{1,0:T(8,128)S(1)}, u32[]{:S(2)}) copy-start(f32[136,384]{1,0:T(8,128)S(1)} %collective-permute-done.1.dn_ref) | copy-start | bytes 626692
